TPU v7x, 256 devices: a whole 4x4x8 slice. The times are simulated.
256 devices in a mesh: section: 2 (over core), expert: 32 (over z, x), dp: 4 (over y).
Axes of the slice: x: 4, y: 4, z: 8, core: 2. Of those that a mesh axis runs over, the one named last changes fastest.
Arguments:
- layer_inputs: bfloat16 [2, 4096, 2048], P('section', 'expert'), may hold values from -6 to 6
- out_grad: bfloat16 [4096, 2048], P('expert'), may hold values from -6 to 6
- expert_ids: int32 [2, 4096, 6], P('section', 'expert'), may hold values from 0 to 63, all different within a row; in each aligned block of 128 rows (0 to 127, 128 to 255, ..., all dimensions but the last counted through in order) at most 16 rows name the same one
- gate_weights: float32 [2, 4096, 6], P('section', 'expert'), may hold values from 0.05 to 0.5
- w_gate: bfloat16 [2, 64, 2048, 1408], P('section', 'expert', None, 'dp'), may hold values from -0.125 to 0.125
- w_up: bfloat16 [2, 64, 2048, 1408], P('section', 'expert', None, 'dp'), may hold values from -0.125 to 0.125
- w_down: bfloat16 [2, 64, 1408, 2048], P('section', 'expert', 'dp'), may hold values from -0.15625 to 0.15625
Outputs:
- input_grads: bfloat16 [2, 4096, 2048], P('section', 'expert')
Inputs may be any that keep to these rules, and one draw needn't show every extreme that they name: `expert_ids`: each row names 6 different experts. In the 128 rows of one index of expert, no expert of a layer is named by more than 16 rows, a bound that some block reaches.
All inputs are finite; a program needn't handle non-finite values.
Results may differ from a plain program's by a relative error of at most 0.006.
Values may be sent and summed in bfloat16 or wider, within the bound.
A program may use at most 128 MiB of HBM per device.

v0:
```python
import jax
import jax.numpy as jnp
from jax import lax
from jax.sharding import PartitionSpec as P


def from_behind(array, axis, by):
    count = lax.axis_size(axis)
    pairs = [(i, i + by) for i in range(count) if 0 <= i + by < count]
    return lax.ppermute(array, axis, pairs)


def silu_parts(pre_gate):
    sig_value = jax.nn.sigmoid(pre_gate)
    return (pre_gate * sig_value, sig_value * (1.0 + pre_gate * (1.0 - sig_value)))


def forward_pre(in_rows, both_mat):
    xlen, slen, clen, dlen = in_rows.shape
    joined = jnp.einsum(
        "xmd,xdf->xmf",
        in_rows.reshape(xlen, slen * clen, dlen),
        both_mat,
        preferred_element_type=jnp.float32,
    )
    half_width = both_mat.shape[2] // 2
    joined = joined.reshape(xlen, slen, clen, -1)
    return (joined[..., :half_width], joined[..., half_width:])


def backward_rows(cot_rows, pre_gate, pre_up, both_mat, down_mat):
    xlen, slen, clen, dlen = cot_rows.shape
    hidden_grad = jnp.einsum(
        "xmd,xfd->xmf",
        cot_rows.reshape(xlen, slen * clen, dlen),
        down_mat,
        preferred_element_type=jnp.float32,
    )
    hidden_grad = hidden_grad.reshape(xlen, slen, clen, -1)
    activation, slope_value = silu_parts(pre_gate)
    gate_grad = (hidden_grad * pre_up * slope_value).astype(jnp.bfloat16)
    up_grad = (hidden_grad * activation).astype(jnp.bfloat16)
    grads = jnp.concatenate([gate_grad, up_grad], axis=3).reshape(xlen, slen * clen, -1)
    partial_value = jnp.einsum("xmf,xdf->xmd", grads, both_mat, preferred_element_type=jnp.float32)
    return partial_value.reshape(xlen, slen, clen, dlen).astype(jnp.bfloat16)


def slot_layout(route_ids, exp_local, owner_count, capacity):
    tok_count, top_count = route_ids.shape
    experts = exp_local * owner_count
    flat_ids = route_ids.reshape(-1)
    hit_table = (flat_ids[:, None] == jnp.arange(experts, dtype=jnp.int32)[None, :]).astype(
        jnp.int32
    )
    before = jnp.cumsum(hit_table, axis=0) - hit_table
    position = jnp.sum(before * hit_table, axis=1)
    target = (flat_ids % exp_local * owner_count + flat_ids // exp_local) * capacity + position
    owners = jnp.arange(tok_count * top_count, dtype=jnp.int32) // top_count
    source = jnp.full((experts * capacity,), tok_count, jnp.int32).at[target].set(owners)
    return (target, source)


def pack_rows(values, source, owner_count, exp_local):
    padded = jnp.concatenate([values, jnp.zeros((1, values.shape[1]), values.dtype)], axis=0)
    picked = jnp.take(padded, source, axis=0)
    return picked.reshape(exp_local, owner_count, -1, values.shape[1])


def dispatch_first(input_send, cot_send, first_work):
    return first_work(
        (
            lax.all_to_all(input_send, "expert", split_axis=1, concat_axis=1, tiled=True),
            lax.all_to_all(cot_send, "expert", split_axis=1, concat_axis=1, tiled=True),
        )
    )


def dispatch_second(cot_send):
    return lax.all_to_all(cot_send, "expert", split_axis=1, concat_axis=1, tiled=True)


def combine(partial_value, target, gate_vals, cotangent):
    tok_count, top_count = gate_vals.shape
    returned = lax.all_to_all(partial_value, "expert", split_axis=1, concat_axis=1, tiled=True)
    col_width = returned.shape[-1]
    per_slot = jnp.take(returned.reshape(-1, col_width), target, axis=0).astype(jnp.float32)
    per_slot = per_slot.reshape(tok_count, top_count, col_width)
    weighted = jnp.sum(per_slot * gate_vals[:, :, None], axis=1)
    dp_total = lax.psum(weighted, "dp")
    return (cotangent.astype(jnp.float32) + dp_total).astype(jnp.bfloat16)


def shards(layer_inputs, out_grad, expert_ids, gate_weights, w_gate, w_up, w_down):
    inputs = layer_inputs[0]
    route_ids = expert_ids[0]
    gate_vals = gate_weights[0]
    both_mat = jnp.concatenate([w_gate[0], w_up[0]], axis=2)
    down_mat = w_down[0]
    tok_count, top_count = route_ids.shape
    exp_local = both_mat.shape[0]
    owner_count = lax.axis_size("expert")
    experts = exp_local * owner_count
    capacity = tok_count * top_count * 4 // (3 * experts)
    target, source = slot_layout(route_ids, exp_local, owner_count, capacity)
    input_send = pack_rows(inputs, source, owner_count, exp_local)
    cot_send = pack_rows(out_grad, source, owner_count, exp_local)

    def first_work(pieces):
        in_rows, cot_rows = pieces
        pre_gate, pre_up = forward_pre(in_rows, both_mat)
        return (pre_gate, pre_up, backward_rows(cot_rows, pre_gate, pre_up, both_mat, down_mat))

    pre_gate, pre_up, partial_value = dispatch_first(input_send, cot_send, first_work)
    first_grad = combine(partial_value, target, gate_vals, out_grad)
    handed = from_behind(first_grad, "section", -1)
    cot_rows = dispatch_second(pack_rows(handed, source, owner_count, exp_local))
    second = backward_rows(cot_rows, pre_gate, pre_up, both_mat, down_mat)
    second_grad = combine(second, target, gate_vals, handed)
    chosen = jnp.where(lax.axis_index("section") == 1, first_grad, second_grad)
    return chosen[None]


def solution(mesh):
    return jax.shard_map(
        shards,
        mesh=mesh,
        in_specs=(
            P("section", "expert", None),
            P("expert", None),
            P("section", "expert", None),
            P("section", "expert", None),
            P("section", "expert", None, "dp"),
            P("section", "expert", None, "dp"),
            P("section", "expert", "dp", None),
        ),
        out_specs=P("section", "expert", None),
        check_vma=False,
    )
```

profile of v0, /device:TPU:2, one launch (start us, length us, event | category | flops | bytes accessed | tf_op | source)
XLA Modules:
  0.0 771.3 jit_solution(9209525086976737637)
XLA Ops:
  10.2 3.4 scatter_custom_fusion
  16.6 9.9 %gather_fusion = bf16[1024,2048]{1,0:T(8,128)(2,1)} fusion(bf16[129,2048]{1,0:T(8,128)(2,1)} %concatenate.18, s32[1024]{0:T(1024)S(1)} %fusion.23), kind=kCustom, calls=%fused_computation.clone | custom fusion | bytes 8392704 | tf_op jit(solution)/shard_map/jit(_take)/gather | solution.py:65
  26.6 6.0 gather_fusion.1
  32.6 5.4 broadcast_select_fusion.1
  40.2 11.7 %all-to-all-start = ((bf16[2,32,16,2048]{3,2,0,1:T(8,128)(2,1)}), bf16[2,32,16,2048]{3,2,0,1:T(8,128)(2,1)}, u32[]{:S(2)}, u32[]{:S(2)}) async-start(bf16[2,32,16,2048]{3,2,0,1:T(8,128)(2,1)} %copy.23), calls=%async_computation | async-start | bytes 8388608 | tf_op jit(solution)/shard_map/all_to_all | solution.py:73
  51.9 4.7 copy.26
  56.6 91.9 %all-to-all-done = bf16[2,32,16,2048]{3,2,0,1:T(8,128)(2,1)} async-done(((bf16[2,32,16,2048]{3,2,0,1:T(8,128)(2,1)}), bf16[2,32,16,2048]{3,2,0,1:T(8,128)(2,1)}, u32[]{:S(2)}, u32[]{:S(2)}) %all-to-all-start) | async-done | bytes 4194336 | tf_op jit(solution)/shard_map/all_to_all | solution.py:73
  148.5 5.4 all-to-all-start.1
  153.9 2.5 copy.24
  156.5 3.5 fusion.2
  160.0 90.6 %all-to-all-done.1 = bf16[2,32,16,2048]{3,2,0,1:T(8,128)(2,1)} async-done(((bf16[2,32,16,2048]{3,2,0,1:T(8,128)(2,1)}), bf16[2,32,16,2048]{3,2,0,1:T(8,128)(2,1)}, u32[]{:S(2)}, u32[]{:S(2)}) %all-to-all-start.1) | async-done | bytes 4194336 | tf_op jit(solution)/shard_map/all_to_all | solution.py:72
  250.6 2.8 copy.27
  254.5 3.5 fusion.4
  260.2 3.7 convolution_convert_fusion.1
  266.2 4.8 all-to-all-start.2
  271.3 96.3 %all-to-all-done.2 = bf16[2,32,16,2048]{3,2,0,1:T(8,128)(2,1)} async-done(((bf16[2,32,16,2048]{3,2,0,1:T(8,128)(2,1)}), bf16[2,32,16,2048]{3,2,0,1:T(8,128)(2,1)}, u32[]{:S(2)}, u32[]{:S(2)}) %all-to-all-start.2) | async-done | bytes 4194336 | tf_op jit(solution)/shard_map/all_to_all | solution.py:84
  367.7 4.7 copy.31
  372.4 9.8 %gather_fusion.2 = bf16[768,2048]{1,0:T(8,128)(2,1)} fusion(bf16[1024,2048]{1,0:T(8,128)(2,1)} %bitcast.52, s32[1024]{0:T(1024)S(1)} %pad_clamp_fusion), kind=kCustom, calls=%fused_computation.1.clone | custom fusion | bytes 6294528 | tf_op jit(solution)/shard_map/jit(_take)/gather | solution.py:86
  382.2 5.1 select_convert_fusion.1
  387.3 7.9 %reshape.222 = f32[128,6,2048]{2,1,0:T(8,128)} reshape(f32[768,2048]{1,0:T(8,128)} %select_convert_fusion.1) | data formatting | bytes 12582912 | tf_op jit(solution)/shard_map/reshape | solution.py:87
  395.1 7.6 multiply_reduce_fusion.1
  402.9 47.4 %all-reduce.6.cloned.1.call-done = f32[128,2048]{1,0:T(8,128)} async-done(((f32[128,2048]{1,0:T(8,128)}), f32[128,2048]{1,0:T(8,128)}) %all-reduce.6.cloned.1.call-update) | async-done | bytes 1048592 | tf_op jit(solution)/shard_map/psum | solution.py:89
  456.3 6.0 gather_fusion.3
  462.3 2.6 broadcast_select_fusion
  465.5 105.9 %all_to_all.25 = bf16[2,32,16,2048]{3,2,0,1:T(8,128)(2,1)S(1)} all-to-all(bf16[2,32,16,2048]{3,2,0,1:T(8,128)(2,1)S(1)} %copy.33), channel_id=1, replica_groups=mesh['section'=2,'expert'=32,'dp'=4] {'expert'}, dimensions={1} | all-to-all | bytes 8388608 | tf_op jit(solution)/shard_map/all_to_all | solution.py:79
  577.4 3.6 convolution_convert_fusion
  581.3 100.1 %all_to_all.26 = bf16[2,32,16,2048]{3,2,0,1:T(8,128)(2,1)S(1)} all-to-all(bf16[2,32,16,2048]{3,2,0,1:T(8,128)(2,1)S(1)} %copy.37), channel_id=1, replica_groups=mesh['section'=2,'expert'=32,'dp'=4] {'expert'}, dimensions={1} | all-to-all | bytes 8388608 | tf_op jit(solution)/shard_map/all_to_all | solution.py:84
  683.7 9.8 %gather_fusion.4 = bf16[768,2048]{1,0:T(8,128)(2,1)} fusion(bf16[1024,2048]{1,0:T(8,128)(2,1)} %bitcast.51, s32[1024]{0:T(1024)S(1)} %pad_clamp_fusion), kind=kCustom, calls=%fused_computation.4.clone | custom fusion | bytes 6294528 | tf_op jit(solution)/shard_map/jit(_take)/gather | solution.py:86
  693.5 5.1 select_convert_fusion
  698.6 7.9 %reshape.224 = f32[128,6,2048]{2,1,0:T(8,128)} reshape(f32[768,2048]{1,0:T(8,128)} %select_convert_fusion) | data formatting | bytes 12582912 | tf_op jit(solution)/shard_map/reshape | solution.py:87
  706.4 7.6 multiply_reduce_fusion
  714.1 47.8 %all-reduce.8.cloned.1.call-done = f32[128,2048]{1,0:T(8,128)} async-done(((f32[128,2048]{1,0:T(8,128)}), f32[128,2048]{1,0:T(8,128)}) %all-reduce.8.cloned.1.call-update) | async-done | bytes 1048592 | tf_op jit(solution)/shard_map/psum | solution.py:89
  (64 shorter events, 32.2 us)
Async XLA Ops:
  6.5 149.9 %copy-start = (bf16[1,2,352,2048]{3,2,1,0:T(8,128)(2,1)S(1)}, bf16[1,2,352,2048]{3,2,1,0:T(8,128)(2,1)}, u32[]{:S(2)}) copy-start(bf16[1,2,352,2048]{3,2,1,0:T(8,128)(2,1)} %param.17) | copy-start | bytes 8650756
  40.2 108.2 %all-to-all-start = ((bf16[2,32,16,2048]{3,2,0,1:T(8,128)(2,1)}), bf16[2,32,16,2048]{3,2,0,1:T(8,128)(2,1)}, u32[]{:S(2)}, u32[]{:S(2)}) async-start(bf16[2,32,16,2048]{3,2,0,1:T(8,128)(2,1)} %copy.23), calls=%async_computation | async-start | bytes 8388608 | tf_op jit(solution)/shard_map/all_to_all | solution.py:73
  148.5 102.1 %all-to-all-start.1 = ((bf16[2,32,16,2048]{3,2,0,1:T(8,128)(2,1)}), bf16[2,32,16,2048]{3,2,0,1:T(8,128)(2,1)}, u32[]{:S(2)}, u32[]{:S(2)}) async-start(bf16[2,32,16,2048]{3,2,0,1:T(8,128)(2,1)} %copy.26), calls=%async_computation.1 | async-start | bytes 8388608 | tf_op jit(solution)/shard_map/all_to_all | solution.py:72
  250.6 3.1 copy-start.9
  250.6 3.9 copy-start.11
  254.5 3.5 copy-start.7
  258.0 1.6 copy-start.1
  266.2 5.0 copy-start.8
  266.2 101.5 %all-to-all-start.2 = ((bf16[2,32,16,2048]{3,2,0,1:T(8,128)(2,1)}), bf16[2,32,16,2048]{3,2,0,1:T(8,128)(2,1)}, u32[]{:S(2)}, u32[]{:S(2)}) async-start(bf16[2,32,16,2048]{3,2,0,1:T(8,128)(2,1)} %copy.30), calls=%async_computation.2 | async-start | bytes 8388608 | tf_op jit(solution)/shard_map/all_to_all | solution.py:84
  271.0 179.3 %all-reduce.6.cloned.1.call-start = ((), (), s32[]{:S(2)}) async-start(), calls=%async_computation.5 | async-start | bytes 2097152 | tf_op jit(solution)/shard_map/psum | solution.py:89
  395.1 55.1 %copy-start.3 = (bf16[128,2048]{1,0:T(8,128)(2,1)S(1)}, bf16[128,2048]{1,0:T(8,128)(2,1)}, u32[]{:S(2)}) copy-start(bf16[128,2048]{1,0:T(8,128)(2,1)} %param.12) | copy-start | bytes 1572868
  402.8 359.0 %all-reduce.8.cloned.1.call-start = ((), (), s32[]{:S(2)}) async-start(), calls=%async_computation.6 | async-start | bytes 2097152 | tf_op jit(solution)/shard_map/psum | solution.py:89
  451.6 1.3 copy-start.4
  451.6 3.8 collective-permute-start
  455.4 0.8 copy-start.6
  572.0 2.3 copy-start.2
  574.4 1.8 copy-start.12
  575.3 2.0 copy-start.10
  706.4 55.4 %copy-start.5 = (bf16[128,2048]{1,0:T(8,128)(2,1)S(1)}, bf16[128,2048]{1,0:T(8,128)(2,1)}, u32[]{:S(2)}) copy-start(bf16[128,2048]{1,0:T(8,128)(2,1)} %copy-done.4) | copy-start | bytes 1572868
Sparse Core Ops, SparseCore 0:
  402.9 47.2 all-reduce.5
  714.2 47.5 all-reduce.7
where the time goes:
time: 777 us; the launch traced here: 771 us
  waiting for transfers between devices  376 us (48%)
  blocking collectives  206 us (27%)
  local copies, waits for them, and re-layouts  92.5 us (12%)
  other arithmetic  42.2 us (5%)
  starting transfers between devices  23.4 us (3%)
  matrix products  16.6 us (2%)
  between operations  14 us (2%)
    all_to_all x1, blocking collectives, dispatch_second(): lax.all_to_all(cot_send, 'expert', split_axis=1, concat_axis=1, tiled=True)  106 us
    all_to_all x1, blocking collectives, combine(): lax.all_to_all(partial_value, 'expert', split_axis=1, concat_axis=1, tile...  100 us
    all_to_all x1, waiting for transfers between devices, combine(): lax.all_to_all(partial_value, 'expert', split_axis=1, concat_axis=1, tile...  96.3 us
    psum x2, waiting for transfers between devices, combine(): dp_total = lax.psum(weighted, 'dp')  95.2 us
    all_to_all x1, waiting for transfers between devices, dispatch_first(): lax.all_to_all(cot_send, 'expert', split_axis=1, concat_axis=1, tiled=True)  91.9 us
    all_to_all x1, waiting for transfers between devices, dispatch_first(): lax.all_to_all(input_send, 'expert', split_axis=1, concat_axis=1, tiled=T...  90.6 us
    gather x3, local copies, waits for them, and re-layouts, pack_rows(): picked = jnp.take(padded, source, axis=0)  21.9 us
    gather x2, local copies, waits for them, and re-layouts, combine(): jnp.take(returned.reshape(-1, col_width), target, axis=0)  19.7 us
  transfers between devices with their start and end apart: 6, of which 6 were waited for; matrix products, arithmetic and copies ran while one was open for 1% of the time, Pallas kernels for 0%

commit v1 on v0

v1 whole, which is shorter than its diff:
```python
import functools

import jax
import jax.numpy as jnp
from jax import lax
from jax.experimental import pallas as pl
from jax.experimental.pallas import tpu as pltpu
from jax.sharding import PartitionSpec as P

BF16 = jnp.bfloat16
F32 = jnp.float32
DIRECTIONS = 2
NT = (((1,), (1,)), ((), ()))


def dot_nn(left, right):
    return jnp.dot(left, right, preferred_element_type=F32)


def dot_nt(left, right):
    return lax.dot_general(left, right, NT, preferred_element_type=F32)


def ring_step(index, count):
    odd = index % 2
    return odd * ((index + 1) // 2) + (1 - odd) * ((count - index // 2) % count)


def kernel(
    sizes,
    x_hbm,
    g_hbm,
    ids_ref,
    gw_ref,
    wg_hbm,
    wu_hbm,
    wd_hbm,
    out_ref,
    xq,
    cq,
    res,
    posn,
    gate_of,
    xs,
    cs,
    rx,
    rc,
    wg,
    wu,
    wd,
    pre_g,
    pre_u,
    part,
    in1,
    in2,
    comb,
    ret,
    acc,
    load_sem,
    xa_send,
    xa_recv,
    ca_send,
    ca_recv,
    xy_send,
    xy_recv,
    cy_send,
    cy_recv,
    r1_send,
    r1_recv,
    r2_send,
    r2_recv,
    back_send,
    back_recv,
    hand_send,
    hand_recv,
    out_send,
    out_recv,
    go_sem,
):
    n_e, n_x, n_q, cap, top = sizes
    n_z = n_e // n_x
    local = wg.shape[0]
    tok, col = xq.shape
    rows = n_e * cap
    group_rows = n_x * cap
    half = rows // 2
    quarter = half // 2
    per_half = n_e // 2
    sec = lax.axis_index("section")
    me = lax.axis_index("expert")
    q = lax.axis_index("dp")
    z, x = me // n_x, me % n_x
    up, down, far = (q + 1) % n_q, (q + n_q - 1) % n_q, (q + 2) % n_q

    def ahead(block):
        dz, dx = ring_step(block // n_x, n_z), block % n_x
        return (z + dz) % n_z * n_x + (x + dx) % n_x

    def behind(block):
        dz, dx = ring_step(block // n_x, n_z), block % n_x
        return (z + n_z - dz) % n_z * n_x + (x + n_x - dx) % n_x

    my_cols = pl.ds(pl.multiple_of(q * col, col), col)
    loads = [
        pltpu.make_async_copy(x_hbm.at[0, :, my_cols], xq, load_sem.at[0]),
        pltpu.make_async_copy(wg_hbm.at[0], wg, load_sem.at[2]),
        pltpu.make_async_copy(wu_hbm.at[0], wu, load_sem.at[3]),
        pltpu.make_async_copy(wd_hbm.at[0], wd, load_sem.at[4]),
    ]
    load_cot = pltpu.make_async_copy(g_hbm.at[:, my_cols], cq, load_sem.at[1])
    loads[0].start()

    @pl.when(sec == 1)
    def _():
        load_cot.start()

    for copy in loads[1:]:
        copy.start()

    barrier = pltpu.get_barrier_semaphore()

    @pl.loop(1, n_e)
    def _(block):
        pl.semaphore_signal(barrier, inc=1, device_id={"expert": ahead(block)})

    for peer in (up, down, far):
        pl.semaphore_signal(barrier, inc=1, device_id={"dp": peer})
    pl.semaphore_signal(barrier, inc=1, device_id={"section": 1 - sec})

    shape = (n_e * local, tok)
    row = lax.broadcasted_iota(jnp.int32, shape, 0)
    block_of, local_of = row // local, row % local
    plane = block_of // n_x
    dz_of = jnp.where(plane % 2 == 1, (plane + 1) // 2, (n_z - plane // 2) % n_z)
    expert_of = ((z + dz_of) % n_z * n_x + (x + block_of % n_x) % n_x) * local + local_of
    named = jnp.zeros(shape, F32)
    weight = jnp.zeros(shape, F32)
    for k in range(top):
        hit = ids_ref[k : k + 1, :] == expert_of
        named = jnp.where(hit, 1.0, named)
        weight = jnp.where(hit, gw_ref[k : k + 1, :], weight)
    earlier = (
        lax.broadcasted_iota(jnp.int32, (tok, tok), 0)
        < lax.broadcasted_iota(jnp.int32, (tok, tok), 1)
    ).astype(F32)
    before = dot_nn(named.astype(BF16), earlier.astype(BF16))
    posn[...] = jnp.where(named > 0.5, before, -1.0)
    gate_of[...] = weight
    step = tok // (local * cap)

    def one_hot(i):
        pos = posn[pl.ds(pl.multiple_of(i * step * local, step * local), step * local), :]
        slot = lax.broadcasted_iota(jnp.int32, (step * local, cap, tok), 1).astype(F32)
        return jnp.where(pos[:, None, :] == slot, 1.0, 0.0)

    def pack(values, packed):
        @pl.loop(0, n_e // step)
        def _(i):
            chosen = one_hot(i).reshape(tok, tok).astype(BF16)
            picked = dot_nn(chosen, values[...]).astype(BF16)
            packed[pl.ds(i * step, step)] = picked.reshape(step, local, cap, col)

    def own_block(packed, rbuf, recv):
        return pltpu.make_async_copy(
            packed.at[0], rbuf.at[q, :, pl.ds(0, cap), :], recv.at[0]
        )

    def spread(packed, rbuf, send, recv, block):
        at = pl.ds(pl.multiple_of(block * cap, cap), cap)
        return pltpu.make_async_remote_copy(
            src_ref=packed.at[block],
            dst_ref=rbuf.at[q, :, at, :],
            send_sem=send.at[block],
            recv_sem=recv.at[block],
            device_id={"expert": ahead(block)},
        )

    def spread_all(packed, rbuf, send, recv):
        own_block(packed, rbuf, recv).start()

        @pl.loop(1, n_e)
        def _(block):
            spread(packed, rbuf, send, recv, block).start()

    def share(rbuf, send, recv, g, way):
        at = pl.ds(pl.multiple_of(g * group_rows, group_rows), group_rows)
        ref = rbuf.at[q, :, at, :]
        return pltpu.make_async_remote_copy(
            src_ref=ref,
            dst_ref=ref,
            send_sem=send.at[way, g],
            recv_sem=recv.at[way, g],
            device_id={"dp": up if way == 0 else down},
        )

    def pass_on(rbuf, send, recv, g, way):
        at = pl.ds(pl.multiple_of(g * group_rows, group_rows), group_rows)
        ref = rbuf.at[down if way == 0 else up, way, at, :]
        return pltpu.make_async_remote_copy(
            src_ref=ref,
            dst_ref=ref,
            send_sem=send.at[2 + way, g],
            recv_sem=recv.at[2 + way, g],
            device_id={"dp": up if way == 0 else down},
        )

    def gather(packed, rbuf, a_send, a_recv, y_send, y_recv):
        def arrive_and_share(g):
            @pl.loop(0, n_x)
            def _(dx):
                block = g * n_x + dx

                @pl.when(block == 0)
                def _():
                    own_block(packed, rbuf, a_recv).wait()

                @pl.when(block > 0)
                def _():
                    spread(packed, rbuf, a_send, a_recv, block).wait_recv()

            for way in range(DIRECTIONS):
                share(rbuf, y_send, y_recv, g, way).start()

        def forward(g):
            for way in range(DIRECTIONS):
                share(rbuf, y_send, y_recv, g, way).wait_recv()
                pass_on(rbuf, y_send, y_recv, g, way).start()

        @pl.loop(0, n_z + 1)
        def _(g):
            @pl.when(g < n_z)
            def _():
                arrive_and_share(g)

            @pl.when(g > 0)
            def _():
                forward(g - 1)

        @pl.loop(0, n_z)
        def _(g):
            for way in range(DIRECTIONS):
                pass_on(rbuf, y_send, y_recv, g, way).wait_recv()

    def drain(packed, rbuf, a_send, a_recv, y_send, y_recv):
        @pl.loop(1, n_e)
        def _(block):
            spread(packed, rbuf, a_send, a_recv, block).wait_send()

        @pl.loop(0, n_z)
        def _(g):
            for way in range(DIRECTIONS):
                share(rbuf, y_send, y_recv, g, way).wait_send()
                pass_on(rbuf, y_send, y_recv, g, way).wait_send()

    x_path = (xs, rx, xa_send, xa_recv)
    c_path = (cs, rc, ca_send, ca_recv)

    loads[0].wait()
    pack(xq, xs)

    @pl.when(sec == 1)
    def _():
        load_cot.wait()
        pack(cq, cs)

    pl.semaphore_wait(barrier, n_e - 1 + 3 + 1)

    def partner_go():
        pl.semaphore_signal(go_sem, inc=1, device_id={"section": 0})

    @pl.when(sec == 0)
    def _():
        pl.semaphore_wait(go_sem, 1)

    spread_all(*x_path)

    @pl.when(sec == 1)
    def _():
        spread_all(*c_path)

    gather(*x_path, xy_send, xy_recv)
    for copy in loads[1:]:
        copy.wait()

    @pl.loop(0, local * 2)
    def _(c):
        l = c // 2
        at = pl.ds(pl.multiple_of(c % 2 * half, half), half)
        for mat, pre in ((wg, pre_g), (wu, pre_u)):
            total = dot_nn(rx[0, l, at, :], mat[l, 0:col, :])
            for p in range(1, n_q):
                total += dot_nn(rx[p, l, at, :], mat[l, p * col : (p + 1) * col, :])
            pre[l, at, :] = total

    def hand_over():
        return pltpu.make_async_remote_copy(
            src_ref=res,
            dst_ref=cq,
            send_sem=hand_send,
            recv_sem=hand_recv,
            device_id={"section": 1 - sec},
        )

    @pl.when(sec == 0)
    def _():
        hand_over().wait_recv()
        pack(cq, cs)
        spread_all(*c_path)

    gather(*c_path, cy_send, cy_recv)

    @pl.when(sec == 1)
    def _():
        partner_go()

    def first_hop(l, h, way):
        at = pl.ds(pl.multiple_of(h * half + way * quarter, quarter), quarter)
        return pltpu.make_async_remote_copy(
            src_ref=part.at[2, l, at, :],
            dst_ref=in1.at[way, l, h],
            send_sem=r1_send.at[way, l, h],
            recv_sem=r1_recv.at[way, l, h],
            device_id={"dp": up if way == 0 else down},
        )

    def second_hop(l, h, way):
        at = pl.ds(pl.multiple_of(h * half, half), half)
        return pltpu.make_async_remote_copy(
            src_ref=part.at[1 if way == 0 else 3, l, at, :],
            dst_ref=in2.at[way, l, h],
            send_sem=r2_send.at[way, l, h],
            recv_sem=r2_recv.at[way, l, h],
            device_id={"dp": up if way == 0 else down},
        )

    def go_back(l, block):
        at = pl.ds(pl.multiple_of(block * cap, cap), cap)
        return pltpu.make_async_remote_copy(
            src_ref=comb.at[l, at, :],
            dst_ref=ret.at[block, l],
            send_sem=back_send.at[l, block],
            recv_sem=back_recv.at[l, block],
            device_id={"expert": behind(block)},
        )

    def stay(l):
        return pltpu.make_async_copy(
            comb.at[l, pl.ds(0, cap), :], ret.at[0, l], back_recv.at[l, 0]
        )

    def stage_compute(c):
        l, h = c // 2, c % 2
        at = pl.ds(pl.multiple_of(h * half, half), half)
        hidden = dot_nt(rc[0, l, at, :], wd[l, :, 0:col])
        for p in range(1, n_q):
            hidden += dot_nt(rc[p, l, at, :], wd[l, :, p * col : (p + 1) * col])
        gate = pre_g[l, at, :]
        sig = jax.nn.sigmoid(gate)
        gate_grad = (hidden * pre_u[l, at, :] * (sig * (1.0 + gate * (1.0 - sig)))).astype(BF16)
        up_grad = (hidden * (gate * sig)).astype(BF16)
        for d in (2, 1, 3, 0):
            cols = pl.ds(pl.multiple_of((q + d) % n_q * col, col), col)
            value = dot_nt(gate_grad, wg[l, cols, :]) + dot_nt(up_grad, wu[l, cols, :])
            part[d, l, at, :] = value.astype(BF16)
            if d == 2:
                for way in range(DIRECTIONS):
                    first_hop(l, h, way).start()

    def stage_add(c):
        l, h = c // 2, c % 2
        for way in range(DIRECTIONS):
            first_hop(l, h, way).wait_recv()
            d = 1 if way == 0 else 3
            at = pl.ds(pl.multiple_of(h * half + way * quarter, quarter), quarter)
            both = part[d, l, at, :].astype(F32) + in1[way, l, h].astype(F32)
            part[d, l, at, :] = both.astype(BF16)
            second_hop(l, h, way).start()

    def stage_back(c):
        l, h = c // 2, c % 2
        at = pl.ds(pl.multiple_of(h * half, half), half)
        for way in range(DIRECTIONS):
            second_hop(l, h, way).wait_recv()
        total = part[0, l, at, :].astype(F32) + in2[0, l, h].astype(F32)
        comb[l, at, :] = (total + in2[1, l, h].astype(F32)).astype(BF16)

        @pl.loop(0, per_half)
        def _(j):
            block = h * per_half + j

            @pl.when(block == 0)
            def _():
                stay(l).start()

            @pl.when(block > 0)
            def _():
                go_back(l, block).start()

    chunks = local * 2

    @pl.loop(0, chunks + 2)
    def _(c):
        @pl.when(c < chunks)
        def _():
            stage_compute(c)

        @pl.when(jnp.logical_and(c >= 1, c < chunks + 1))
        def _():
            stage_add(c - 1)

        @pl.when(c >= 2)
        def _():
            stage_back(c - 2)

    @pl.loop(0, local)
    def _(l):
        stay(l).wait()

        @pl.loop(1, n_e)
        def _(block):
            go_back(l, block).wait_recv()

    acc[...] = cq[...].astype(F32)

    @pl.loop(0, n_e // step)
    def _(i):
        weight = gate_of[pl.ds(pl.multiple_of(i * step * local, step * local), step * local), :]
        placed = (one_hot(i) * weight[:, None, :]).reshape(tok, tok).T
        rows_in = ret[pl.ds(i * step, step)].reshape(tok, col)
        high = placed.astype(BF16)
        rest = placed - high.astype(F32)
        middle = rest.astype(BF16)
        low = (rest - middle.astype(F32)).astype(BF16)
        acc[...] += dot_nn(high, rows_in) + (dot_nn(middle, rows_in) + dot_nn(low, rows_in))

    res[...] = acc[...].astype(BF16)

    @pl.when(sec == 1)
    def _():
        hand_over().start()

    def publish(index, peer):
        return pltpu.make_async_remote_copy(
            src_ref=res,
            dst_ref=out_ref.at[0, :, my_cols],
            send_sem=out_send.at[index],
            recv_sem=out_recv.at[index],
            device_id={"dp": peer},
        )

    shares = [publish(i, peer) for i, peer in enumerate((up, down, far))]
    for copy in shares:
        copy.start()
    out_ref[0, :, my_cols] = res[...]

    drain(*x_path, xy_send, xy_recv)
    drain(*c_path, cy_send, cy_recv)

    @pl.loop(0, local)
    def _(l):
        for h in range(2):
            for way in range(DIRECTIONS):
                first_hop(l, h, way).wait_send()
                second_hop(l, h, way).wait_send()

        @pl.loop(1, n_e)
        def _(block):
            go_back(l, block).wait_send()

    for copy in shares:
        copy.wait()

    @pl.when(sec == 1)
    def _():
        hand_over().wait_send()


def shards(n_x, layer_inputs, out_grad, expert_ids, gate_weights, w_gate, w_up, w_down):
    n_e, n_q = lax.axis_size("expert"), lax.axis_size("dp")
    _, tok, width = layer_inputs.shape
    _, local, _, hidden = w_gate.shape
    top = expert_ids.shape[2]
    cap = tok * top * 4 // (3 * local * n_e)
    col = width // n_q
    rows = n_e * cap
    n_z = n_e // n_x
    dma = pltpu.SemaphoreType.DMA
    scratch = [
        pltpu.VMEM((tok, col), BF16),
        pltpu.VMEM((tok, col), BF16),
        pltpu.VMEM((tok, col), BF16),
        pltpu.VMEM((n_e * local, tok), F32),
        pltpu.VMEM((n_e * local, tok), F32),
        pltpu.VMEM((n_e, local, cap, col), BF16),
        pltpu.VMEM((n_e, local, cap, col), BF16),
        pltpu.VMEM((n_q, local, rows, col), BF16),
        pltpu.VMEM((n_q, local, rows, col), BF16),
        pltpu.VMEM((local, width, hidden), BF16),
        pltpu.VMEM((local, width, hidden), BF16),
        pltpu.VMEM((local, hidden, width), BF16),
        pltpu.VMEM((local, rows, hidden), F32),
        pltpu.VMEM((local, rows, hidden), F32),
        pltpu.VMEM((n_q, local, rows, col), BF16),
        pltpu.VMEM((DIRECTIONS, local, 2, rows // 4, col), BF16),
        pltpu.VMEM((DIRECTIONS, local, 2, rows // 2, col), BF16),
        pltpu.VMEM((local, rows, col), BF16),
        pltpu.VMEM((n_e, local, cap, col), BF16),
        pltpu.VMEM((tok, col), F32),
        dma((5,)),
        dma((n_e,)),
        dma((n_e,)),
        dma((n_e,)),
        dma((n_e,)),
        dma((4, n_z)),
        dma((4, n_z)),
        dma((4, n_z)),
        dma((4, n_z)),
        dma((DIRECTIONS, local, 2)),
        dma((DIRECTIONS, local, 2)),
        dma((DIRECTIONS, local, 2)),
        dma((DIRECTIONS, local, 2)),
        dma((local, n_e)),
        dma((local, n_e)),
        dma,
        dma,
        dma((3,)),
        dma((3,)),
        pltpu.SemaphoreType.REGULAR,
    ]
    vmem, anywhere = pl.BlockSpec(memory_space=pltpu.VMEM), pl.BlockSpec(memory_space=pl.ANY)
    return pl.pallas_call(
        functools.partial(kernel, (n_e, n_x, n_q, cap, top)),
        out_shape=jax.ShapeDtypeStruct((1, tok, width), BF16),
        in_specs=[anywhere, anywhere, vmem, vmem, anywhere, anywhere, anywhere],
        out_specs=vmem,
        scratch_shapes=scratch,
        compiler_params=pltpu.CompilerParams(
            collective_id=0, has_side_effects=True, vmem_limit_bytes=56 * 1024 * 1024
        ),
        name="routed_input_grads",
    )(
        layer_inputs,
        out_grad,
        expert_ids[0].T,
        gate_weights[0].T,
        w_gate,
        w_up,
        w_down,
    )


def solution(mesh):
    n_x = 4 if mesh.shape["expert"] % 8 == 0 else 2
    return jax.shard_map(
        functools.partial(shards, n_x),
        mesh=mesh,
        in_specs=(
            P("section", "expert", None),
            P("expert", None),
            P("section", "expert", None),
            P("section", "expert", None),
            P("section", "expert", None, "dp"),
            P("section", "expert", None, "dp"),
            P("section", "expert", "dp", None),
        ),
        out_specs=P("section", "expert", None),
        check_vma=False,
    )
```

time: 777 us -> 203 us (0.26)
  waiting for transfers between devices: 376 us -> 0 us
  blocking collectives: 206 us -> 0 us
  Pallas kernels: 0 us -> 189 us
  local copies, waits for them, and re-layouts: 92.5 us -> 12 us
  other arithmetic: 42.2 us -> 0 us
  starting transfers between devices: 23.4 us -> 0 us
  matrix products: 16.6 us -> 0 us
  between operations: 14 us -> 0.01 us
    all_to_all x3 -> x0, waiting for transfers between devices: 279 us -> none  [the longest x1 96.3 us: combine(): lax.all_to_all(partial_value, 'expert', split_axis=1, concat_axis=1, tile...]
    all_to_all x2 -> x0, blocking collectives: 206 us -> none  [the longest x1 106 us: dispatch_second(): lax.all_to_all(cot_send, 'expert', split_axis=1, concat_axis=1, tiled=True)]
    pallas_call x0 -> x1, Pallas kernels: none -> 189 us  [shards(): pl.pallas_call(functools.partial(kernel, (n_e, n_x, n_q, cap, top)), out_...]
    psum x2 -> x0, waiting for transfers between devices: 95.2 us -> none  [combine(): dp_total = lax.psum(weighted, 'dp')]
    gather x5 -> x0, local copies, waits for them, and re-layouts: 41.6 us -> none  [the longest x3 21.9 us: pack_rows(): picked = jnp.take(padded, source, axis=0)]
    reshape x5 -> x0, local copies, waits for them, and re-layouts: 23.3 us -> none  [the longest x2 15.7 us: combine(): per_slot = per_slot.reshape(tok_count, top_count, col_width)]
    all_to_all x3 -> x0, starting transfers between devices: 21.9 us -> none  [the longest x1 11.7 us: dispatch_first(): lax.all_to_all(cot_send, 'expert', split_axis=1, concat_axis=1, tiled=True)]
    dot_general x5 -> x0, matrix products: 16.6 us -> none  [the longest x2 7.32 us: backward_rows(): jnp.einsum('xmf,xdf->xmd', grads, both_mat, preferred_element_type=jnp.fl...]
  transfers between devices with their start and end apart: 6 -> 0, of which waited for: 6 -> 0; matrix products, arithmetic and copies ran while one was open for 1% -> 0% of each run, Pallas kernels for 0% -> 0%
where the time goes in v1:
time: 203 us; the launch traced here: 201 us
  Pallas kernels  189 us (93%)
  local copies, waits for them, and re-layouts  12 us (6%)
    pallas_call x1, Pallas kernels, shards(): pl.pallas_call(functools.partial(kernel, (n_e, n_x, n_q, cap, top)), out_...  189 us
    unnamed x7, local copies, waits for them, and re-layouts  12 us

profile of v1, /device:TPU:2, one launch (start us, length us, event | category | flops | bytes accessed | tf_op | source)
XLA Modules:
  0.0 200.9 jit_solution(4052065984310650058)
XLA Ops:
  0.0 1.3 copy.15
  1.3 1.3 copy.14
  2.5 0.0 copy-start
  2.5 4.7 %copy.8.wg_hbm = bf16[1,2,2048,352]{3,2,1,0:T(8,128)(2,1)} copy(bf16[1,2,2048,352]{2,3,1,0:T(8,128)(2,1)} %param.11) | data formatting | bytes 5767168 | tf_op args[4]
  7.3 0.0 copy-done
  7.3 2.8 %copy.9.wu_hbm = bf16[1,2,2048,352]{3,2,1,0:T(8,128)(2,1)} copy(bf16[1,2,2048,352]{2,3,1,0:T(8,128)(2,1)S(1)} %copy-done) | data formatting | bytes 5767168 | tf_op args[5]
  10.1 188.9 %routed_input_grads.1 = bf16[1,128,2048]{2,1,0:T(8,128)(2,1)} custom-call(bf16[1,128,2048]{2,1,0:T(8,128)(2,1)} %x_hbm.1, bf16[128,2048]{1,0:T(8,128)(2,1)} %g_hbm.1, s32[6,128]{1,0:T(8,128)} %bitcast.10, f32[6,128]{1,0:T(8,128)} %bitcast.11, bf16[1,2,2048,352]{3,2,1,0:T(8,128)(2,1)} %copy.8.wg_hbm, bf16[1,2,2048,352]{3,2,1,0:T(8,128)(2,1)} %copy.9.wu_hbm, ...), custom_call_target="tpu_custom_call" | custom-call | tf_op jit(solution)/shard_map/routed_input_grads/pallas_call | solution.py:531
  199.0 1.9 copy.17
Async XLA Ops:
  2.5 4.8 %copy-start = (bf16[1,2,2048,352]{2,3,1,0:T(8,128)(2,1)S(1)}, bf16[1,2,2048,352]{2,3,1,0:T(8,128)(2,1)}, u32[]{:S(2)}) copy-start(bf16[1,2,2048,352]{2,3,1,0:T(8,128)(2,1)} %param.12) | copy-start | bytes 8650756

commit v2 on v1

--- a/solution.py
+++ b/solution.py
@@ -11,6 +11,8 @@
 F32 = jnp.float32
 DIRECTIONS = 2
 NT = (((1,), (1,)), ((), ()))
+PRE_AT = 1
+GO_AT = (0, 3)
 
 
 def dot_nn(left, right):
@@ -45,11 +47,9 @@
     cs,
     rx,
     rc,
-    wg,
-    wu,
+    wgu,
     wd,
-    pre_g,
-    pre_u,
+    pre,
     part,
     in1,
     in2,
@@ -79,7 +79,8 @@
 ):
     n_e, n_x, n_q, cap, top = sizes
     n_z = n_e // n_x
-    local = wg.shape[0]
+    local = wd.shape[0]
+    hidden, padded = wd_hbm.shape[2], wd.shape[1]
     tok, col = xq.shape
     rows = n_e * cap
     group_rows = n_x * cap
@@ -103,9 +104,9 @@
     my_cols = pl.ds(pl.multiple_of(q * col, col), col)
     loads = [
         pltpu.make_async_copy(x_hbm.at[0, :, my_cols], xq, load_sem.at[0]),
-        pltpu.make_async_copy(wg_hbm.at[0], wg, load_sem.at[2]),
-        pltpu.make_async_copy(wu_hbm.at[0], wu, load_sem.at[3]),
-        pltpu.make_async_copy(wd_hbm.at[0], wd, load_sem.at[4]),
+        pltpu.make_async_copy(wg_hbm.at[0], wgu.at[:, 0:hidden, :], load_sem.at[2]),
+        pltpu.make_async_copy(wu_hbm.at[0], wgu.at[:, padded : padded + hidden, :], load_sem.at[3]),
+        pltpu.make_async_copy(wd_hbm.at[0], wd.at[:, 0:hidden, :], load_sem.at[4]),
     ]
     load_cot = pltpu.make_async_copy(g_hbm.at[:, my_cols], cq, load_sem.at[1])
     loads[0].start()
@@ -126,6 +127,12 @@
     for peer in (up, down, far):
         pl.semaphore_signal(barrier, inc=1, device_id={"dp": peer})
     pl.semaphore_signal(barrier, inc=1, device_id={"section": 1 - sec})
+
+    if padded > hidden:
+        none = jnp.zeros((local, padded - hidden, wd.shape[2]), BF16)
+        wgu[:, hidden:padded, :] = none
+        wgu[:, padded + hidden :, :] = none
+        wd[:, hidden:, :] = none
 
     shape = (n_e * local, tok)
     row = lax.broadcasted_iota(jnp.int32, shape, 0)
@@ -136,9 +143,9 @@
     named = jnp.zeros(shape, F32)
     weight = jnp.zeros(shape, F32)
     for k in range(top):
-        hit = ids_ref[k : k + 1, :] == expert_of
+        hit = ids_ref[k] == expert_of
         named = jnp.where(hit, 1.0, named)
-        weight = jnp.where(hit, gw_ref[k : k + 1, :], weight)
+        weight = jnp.where(hit, gw_ref[k], weight)
     earlier = (
         lax.broadcasted_iota(jnp.int32, (tok, tok), 0)
         < lax.broadcasted_iota(jnp.int32, (tok, tok), 1)
@@ -204,42 +211,32 @@
             device_id={"dp": up if way == 0 else down},
         )
 
-    def gather(packed, rbuf, a_send, a_recv, y_send, y_recv):
-        def arrive_and_share(g):
-            @pl.loop(0, n_x)
-            def _(dx):
-                block = g * n_x + dx
-
-                @pl.when(block == 0)
-                def _():
-                    own_block(packed, rbuf, a_recv).wait()
-
-                @pl.when(block > 0)
-                def _():
-                    spread(packed, rbuf, a_send, a_recv, block).wait_recv()
-
+    def arrive_and_share(packed, rbuf, a_send, a_recv, y_send, y_recv, g):
+        @pl.loop(0, n_x)
+        def _(dx):
+            block = g * n_x + dx
+
+            @pl.when(block == 0)
+            def _():
+                own_block(packed, rbuf, a_recv).wait()
+
+            @pl.when(block > 0)
+            def _():
+                spread(packed, rbuf, a_send, a_recv, block).wait_recv()
+
+        for way in range(DIRECTIONS):
+            share(rbuf, y_send, y_recv, g, way).start()
+
+    def forward(rbuf, y_send, y_recv, g):
+        for way in range(DIRECTIONS):
+            share(rbuf, y_send, y_recv, g, way).wait_recv()
+            pass_on(rbuf, y_send, y_recv, g, way).start()
+
+    def settle(rbuf, y_send, y_recv, h):
+        @pl.loop(0, n_z // 2)
+        def _(i):
             for way in range(DIRECTIONS):
-                share(rbuf, y_send, y_recv, g, way).start()
-
-        def forward(g):
-            for way in range(DIRECTIONS):
-                share(rbuf, y_send, y_recv, g, way).wait_recv()
-                pass_on(rbuf, y_send, y_recv, g, way).start()
-
-        @pl.loop(0, n_z + 1)
-        def _(g):
-            @pl.when(g < n_z)
-            def _():
-                arrive_and_share(g)
-
-            @pl.when(g > 0)
-            def _():
-                forward(g - 1)
-
-        @pl.loop(0, n_z)
-        def _(g):
-            for way in range(DIRECTIONS):
-                pass_on(rbuf, y_send, y_recv, g, way).wait_recv()
+                pass_on(rbuf, y_send, y_recv, h * (n_z // 2) + i, way).wait_recv()
 
     def drain(packed, rbuf, a_send, a_recv, y_send, y_recv):
         @pl.loop(1, n_e)
@@ -265,12 +262,11 @@
 
     pl.semaphore_wait(barrier, n_e - 1 + 3 + 1)
 
-    def partner_go():
-        pl.semaphore_signal(go_sem, inc=1, device_id={"section": 0})
+    x_y, c_y = (xy_send, xy_recv), (cy_send, cy_recv)
 
     @pl.when(sec == 0)
     def _():
-        pl.semaphore_wait(go_sem, 1)
+        pl.semaphore_wait(go_sem.at[0], 1)
 
     spread_all(*x_path)
 
@@ -278,19 +274,37 @@
     def _():
         spread_all(*c_path)
 
-    gather(*x_path, xy_send, xy_recv)
+    @pl.when(sec == 0)
+    def _():
+        pl.semaphore_wait(go_sem.at[1], 1)
+
+    @pl.loop(0, n_z + 1)
+    def _(g):
+        @pl.when(g < n_z)
+        def _():
+            arrive_and_share(*x_path, *x_y, g)
+
+        @pl.when(g > 0)
+        def _():
+            forward(rx, *x_y, g - 1)
+
     for copy in loads[1:]:
         copy.wait()
 
-    @pl.loop(0, local * 2)
-    def _(c):
-        l = c // 2
-        at = pl.ds(pl.multiple_of(c % 2 * half, half), half)
-        for mat, pre in ((wg, pre_g), (wu, pre_u)):
-            total = dot_nn(rx[0, l, at, :], mat[l, 0:col, :])
-            for p in range(1, n_q):
-                total += dot_nn(rx[p, l, at, :], mat[l, p * col : (p + 1) * col, :])
-            pre[l, at, :] = total
+    chunks = local * 2
+
+    def stage_pre(c):
+        h, l = c // local, c % local
+
+        @pl.when(l == 0)
+        def _():
+            settle(rx, *x_y, h)
+
+        at = pl.ds(pl.multiple_of(h * half, half), half)
+        total = dot_nt(rx[0, l, at, :], wgu[l, :, 0:col])
+        for p in range(1, n_q):
+            total += dot_nt(rx[p, l, at, :], wgu[l, :, p * col : (p + 1) * col])
+        pre[l, at, :] = total
 
     def hand_over():
         return pltpu.make_async_remote_copy(
@@ -303,15 +317,13 @@
 
     @pl.when(sec == 0)
     def _():
+        @pl.loop(0, chunks)
+        def _(c):
+            stage_pre(c)
+
         hand_over().wait_recv()
         pack(cq, cs)
         spread_all(*c_path)
-
-    gather(*c_path, cy_send, cy_recv)
-
-    @pl.when(sec == 1)
-    def _():
-        partner_go()
 
     def first_hop(l, h, way):
         at = pl.ds(pl.multiple_of(h * half + way * quarter, quarter), quarter)
@@ -349,25 +361,30 @@
         )
 
     def stage_compute(c):
-        l, h = c // 2, c % 2
+        h, l = c // local, c % local
+
+        @pl.when(l == 0)
+        def _():
+            settle(rc, *c_y, h)
+
         at = pl.ds(pl.multiple_of(h * half, half), half)
-        hidden = dot_nt(rc[0, l, at, :], wd[l, :, 0:col])
+        hidden_grad = dot_nt(rc[0, l, at, :], wd[l, :, 0:col])
         for p in range(1, n_q):
-            hidden += dot_nt(rc[p, l, at, :], wd[l, :, p * col : (p + 1) * col])
-        gate = pre_g[l, at, :]
+            hidden_grad += dot_nt(rc[p, l, at, :], wd[l, :, p * col : (p + 1) * col])
+        gate, up_value = pre[l, at, 0:padded], pre[l, at, padded:]
         sig = jax.nn.sigmoid(gate)
-        gate_grad = (hidden * pre_u[l, at, :] * (sig * (1.0 + gate * (1.0 - sig)))).astype(BF16)
-        up_grad = (hidden * (gate * sig)).astype(BF16)
+        gate_grad = (hidden_grad * up_value * (sig * (1.0 + gate * (1.0 - sig)))).astype(BF16)
+        up_grad = (hidden_grad * (gate * sig)).astype(BF16)
+        grads = jnp.concatenate([gate_grad, up_grad], axis=1)
         for d in (2, 1, 3, 0):
             cols = pl.ds(pl.multiple_of((q + d) % n_q * col, col), col)
-            value = dot_nt(gate_grad, wg[l, cols, :]) + dot_nt(up_grad, wu[l, cols, :])
-            part[d, l, at, :] = value.astype(BF16)
+            part[d, l, at, :] = dot_nn(grads, wgu[l, :, cols]).astype(BF16)
             if d == 2:
                 for way in range(DIRECTIONS):
                     first_hop(l, h, way).start()
 
     def stage_add(c):
-        l, h = c // 2, c % 2
+        h, l = c // local, c % local
         for way in range(DIRECTIONS):
             first_hop(l, h, way).wait_recv()
             d = 1 if way == 0 else 3
@@ -377,7 +394,7 @@
             second_hop(l, h, way).start()
 
     def stage_back(c):
-        l, h = c // 2, c % 2
+        h, l = c // local, c % local
         at = pl.ds(pl.multiple_of(h * half, half), half)
         for way in range(DIRECTIONS):
             second_hop(l, h, way).wait_recv()
@@ -396,21 +413,44 @@
             def _():
                 go_back(l, block).start()
 
-    chunks = local * 2
-
-    @pl.loop(0, chunks + 2)
-    def _(c):
-        @pl.when(c < chunks)
-        def _():
-            stage_compute(c)
-
-        @pl.when(jnp.logical_and(c >= 1, c < chunks + 1))
-        def _():
-            stage_add(c - 1)
-
-        @pl.when(c >= 2)
-        def _():
-            stage_back(c - 2)
+    def within(t, low, count):
+        return jnp.logical_and(t >= low, t < low + count)
+
+    first = n_z - 1
+
+    @pl.loop(0, first + chunks + 2)
+    def _(t):
+        @pl.when(t < n_z)
+        def _():
+            arrive_and_share(*c_path, *c_y, t)
+
+        @pl.when(within(t, 1, n_z))
+        def _():
+            forward(rc, *c_y, t - 1)
+
+        @pl.when(jnp.logical_and(sec == 1, within(t, PRE_AT, chunks)))
+        def _():
+            stage_pre(t - PRE_AT)
+
+        @pl.when(jnp.logical_and(sec == 1, t == GO_AT[0]))
+        def _():
+            pl.semaphore_signal(go_sem.at[0], inc=1, device_id={"section": 0})
+
+        @pl.when(within(t, first, chunks))
+        def _():
+            stage_compute(t - first)
+
+        @pl.when(within(t, first + 1, chunks))
+        def _():
+            stage_add(t - first - 1)
+
+        @pl.when(within(t, first + 2, chunks))
+        def _():
+            stage_back(t - first - 2)
+
+        @pl.when(jnp.logical_and(sec == 1, t == first + GO_AT[1]))
+        def _():
+            pl.semaphore_signal(go_sem.at[1], inc=1, device_id={"section": 0})
 
     @pl.loop(0, local)
     def _(l):
@@ -484,6 +524,7 @@
     col = width // n_q
     rows = n_e * cap
     n_z = n_e // n_x
+    padded = -(-hidden // 128) * 128
     dma = pltpu.SemaphoreType.DMA
     scratch = [
         pltpu.VMEM((tok, col), BF16),
@@ -495,11 +536,9 @@
         pltpu.VMEM((n_e, local, cap, col), BF16),
         pltpu.VMEM((n_q, local, rows, col), BF16),
         pltpu.VMEM((n_q, local, rows, col), BF16),
-        pltpu.VMEM((local, width, hidden), BF16),
-        pltpu.VMEM((local, width, hidden), BF16),
-        pltpu.VMEM((local, hidden, width), BF16),
-        pltpu.VMEM((local, rows, hidden), F32),
-        pltpu.VMEM((local, rows, hidden), F32),
+        pltpu.VMEM((local, 2 * padded, width), BF16),
+        pltpu.VMEM((local, padded, width), BF16),
+        pltpu.VMEM((local, rows, 2 * padded), F32),
         pltpu.VMEM((n_q, local, rows, col), BF16),
         pltpu.VMEM((DIRECTIONS, local, 2, rows // 4, col), BF16),
         pltpu.VMEM((DIRECTIONS, local, 2, rows // 2, col), BF16),
@@ -525,7 +564,7 @@
         dma,
         dma((3,)),
         dma((3,)),
-        pltpu.SemaphoreType.REGULAR,
+        pltpu.SemaphoreType.REGULAR((2,)),
     ]
     vmem, anywhere = pl.BlockSpec(memory_space=pltpu.VMEM), pl.BlockSpec(memory_space=pl.ANY)
     return pl.pallas_call(
@@ -541,10 +580,10 @@
     )(
         layer_inputs,
         out_grad,
-        expert_ids[0].T,
-        gate_weights[0].T,
-        w_gate,
-        w_up,
+        jnp.transpose(expert_ids, (2, 0, 1)),
+        jnp.transpose(gate_weights, (2, 0, 1)),
+        jnp.swapaxes(w_gate, 2, 3),
+        jnp.swapaxes(w_up, 2, 3),
         w_down,
     )
 

time: 203 us -> 176 us (0.87); the launches traced: 201 us -> 176 us
  Pallas kernels: 189 us -> 174 us
  local copies, waits for them, and re-layouts: 12 us -> 1.88 us
    pallas_call x1, Pallas kernels: 189 us -> 174 us  [shards(): pl.pallas_call(functools.partial(kernel, (n_e, n_x, n_q, cap, top)), out_...]
    unnamed x7 -> x1, local copies, waits for them, and re-layouts: 12 us -> 1.88 us
where the time goes in v2:
time: 176 us
  Pallas kernels  174 us (99%)
  local copies, waits for them, and re-layouts  1.88 us (1%)
    pallas_call x1, Pallas kernels, shards(): pl.pallas_call(functools.partial(kernel, (n_e, n_x, n_q, cap, top)), out_...  174 us

profile of v2, /device:TPU:2, one launch (start us, length us, event | category | flops | bytes accessed | tf_op | source)
XLA Modules:
  0.0 176.3 jit_solution(15693096115513667962)
XLA Ops:
  0.0 174.4 %routed_input_grads.1 = bf16[1,128,2048]{2,1,0:T(8,128)(2,1)} custom-call(bf16[1,128,2048]{2,1,0:T(8,128)(2,1)} %x_hbm.1, bf16[128,2048]{1,0:T(8,128)(2,1)} %g_hbm.1, s32[6,1,128]{2,1,0:T(1,128)} %bitcast.6, f32[6,1,128]{2,1,0:T(1,128)} %bitcast.7, bf16[1,2,352,2048]{3,2,1,0:T(8,128)(2,1)} %bitcast.4, bf16[1,2,352,2048]{3,2,1,0:T(8,128)(2,1)} %bitcast.5, ...), custom_call_target="tpu_custom_call" | custom-call | tf_op jit(solution)/shard_map/routed_input_grads/pallas_call | solution.py:570
  174.4 1.9 %copy.9 = bf16[1,128,2048]{2,1,0:T(8,128)(2,1)} copy(bf16[1,128,2048]{2,1,0:T(8,128)(2,1)} %routed_input_grads.1) | data formatting | bytes 1048576
